TPU v7x, 256 devices: a whole 4x4x8 slice. The times are simulated.
256 devices in a mesh: seq: 128 (over z, x, y_lo, core), sec: 2 (over y_hi).
Axes of the slice: x: 4, y: 4 (y_hi: 2, y_lo: 2; y = y_hi * 2 + y_lo), z: 8, core: 2. Of those that a mesh axis runs over, the one named last changes fastest.
Arguments:
- queries: bfloat16 [2, 2048, 64, 3072], P('sec', 'seq'), may hold values from -250 to 250
- encoded: bfloat16 [2, 1024, 32, 512], P('sec', 'seq'), may hold values from -6 to 6
- neighbours: int32 [2, 2048, 2], P('sec', 'seq'), may hold values from 0 to 1023, as said below
- kv_weight: bfloat16 [2, 512, 3072], P(None, None, 'seq'), may hold values from -0.25 to 0.25
Outputs:
- attended: bfloat16 [2, 2048, 64, 3072], P('sec', 'seq')
Inputs may be any that keep to these rules, and one draw needn't show every extreme that they name: Block id b lies on index b // 8 of seq. The spans held by one device of seq name at most 1 neighbours on any one index of seq, and in every draw some indices of seq receive exactly 1 from every device.
All inputs are finite; a program needn't handle non-finite values.
Results may differ from a plain program's by a relative error of at most 0.012.
Values may be sent and summed in bfloat16 or wider, within the bound.
No kernel may reach another device: no remote copies, remote signals or barrier semaphores. Data moves between devices by JAX's collectives and lax.ppermute only.
A program may use at most 128 MiB of HBM per device.

v0:
```python
import jax
import jax.numpy as jnp
from jax import lax
from jax.sharding import PartitionSpec as P

HDIM = 128


def from_partner(shard, axis, distance):
    return lax.ppermute(shard, axis, [(i, i ^ 1 << distance) for i in range(lax.axis_size(axis))])


def fetch_rows(block_ids, store, owners, slots_each, blocks_each):
    owner = block_ids // blocks_each
    local = block_ids % blocks_each
    owner_match = (owner[:, None] == jnp.arange(owners)[None, :]).astype(jnp.int32)
    rank = jnp.sum(jnp.cumsum(owner_match, 0) * owner_match, 1) - 1
    slot = owner * slots_each + rank
    placed = (slot[:, None] == jnp.arange(owners * slots_each)[None, :]).astype(jnp.int32)
    request = jnp.sum(placed * local[:, None], 0).reshape(owners, slots_each)
    asked = lax.all_to_all(request, "seq", split_axis=0, concat_axis=0, tiled=True)
    rows = store[asked.reshape(-1)].reshape(asked.shape + store.shape[1:])
    replies = lax.all_to_all(rows, "seq", split_axis=0, concat_axis=0, tiled=True)
    flat = replies.reshape((owners * slots_each,) + store.shape[1:])
    return flat[slot]


def body(queries, encoded, neighbours, kv_weight):
    owners = lax.axis_size("seq")
    span_count = queries.shape[1]
    blocks_each = encoded.shape[1]
    token_count = encoded.shape[2]
    width = encoded.shape[3]
    slots_each = (2 * span_count + owners - 1) // owners
    store = encoded[0]
    block_ids = neighbours[0].reshape(-1)
    remote = from_partner(store, "sec", 0)
    fetched = fetch_rows(block_ids, remote, owners, slots_each, blocks_each)
    rows = fetched.reshape(-1, width)
    piece = lax.all_gather(kv_weight, "seq", axis=2, tiled=True)
    keys = jnp.dot(rows, piece[0], preferred_element_type=jnp.float32).astype(jnp.bfloat16)
    values = jnp.dot(rows, piece[1], preferred_element_type=jnp.float32).astype(jnp.bfloat16)
    projected = jnp.stack([keys, values])
    features = queries.shape[3]
    heads = features // HDIM
    keys = projected[0].reshape(span_count, 2 * token_count, heads, HDIM)
    values = projected[1].reshape(span_count, 2 * token_count, heads, HDIM)
    query_block = queries[0].reshape(span_count, queries.shape[2], heads, HDIM)
    scores = jnp.einsum(
        "cthd,cuhd->chtu", query_block, keys, preferred_element_type=jnp.float32
    ) * HDIM ** (-0.5)
    probs = jax.nn.softmax(scores, axis=-1).astype(jnp.bfloat16)
    mixed = jnp.einsum("chtu,cuhd->cthd", probs, values, preferred_element_type=jnp.float32)
    return mixed.astype(jnp.bfloat16).reshape(1, span_count, queries.shape[2], features)


def solution(mesh):
    placed = (
        P("sec", "seq", None, None),
        P("sec", "seq", None, None),
        P("sec", "seq", None),
        P(None, None, "seq"),
    )
    return jax.shard_map(
        body, mesh=mesh, in_specs=placed, out_specs=P("sec", "seq", None, None), check_vma=False
    )
```

profile of v0, /device:TPU:1, one launch (start us, length us, event | category | flops | bytes accessed | tf_op | source)
XLA Modules:
  0.0 335.6 jit_solution(252661657235599470)
XLA Ops:
  6.5 0.0 all-gather.2.cloned.1.call-start
  6.5 0.7 all-gather.2.cloned.1.call-update
  7.3 0.8 copy.26
  8.0 0.1 reshape_squeeze.8
  8.1 0.1 fusion.15
  8.2 0.1 reduce_window_sum.11
  8.2 0.2 select_reduce_fusion.1
  8.4 0.1 select_reduce_fusion
  8.5 0.8 copy.27
  9.3 14.8 %all-to-all-start = ((s32[128,1,1]{2,1,0:T(1,128)}), s32[128,1,1]{2,1,0:T(1,128)S(1)}, u32[]{:S(2)}, u32[]{:S(2)}) async-start(s32[128,1,1]{2,1,0:T(1,128)} %copy.27), calls=%async_computation | async-start | bytes 131072 | tf_op jit(solution)/shard_map/all_to_all | solution.py:21
  24.1 2.7 collective-permute-start
  26.8 7.5 %all-to-all-done = s32[128,1,1]{2,1,0:T(1,128)S(1)} async-done(((s32[128,1,1]{2,1,0:T(1,128)}), s32[128,1,1]{2,1,0:T(1,128)S(1)}, u32[]{:S(2)}, u32[]{:S(2)}) %all-to-all-start) | async-done | bytes 544 | tf_op jit(solution)/shard_map/all_to_all | solution.py:21
  34.2 2.3 reduce
  36.6 0.0 collective-permute-done
  36.6 2.9 gather_fusion
  39.5 11.4 %all-to-all-start.1 = ((bf16[128,1,32,512]{3,2,1,0:T(8,128)(2,1)}), bf16[128,1,32,512]{3,2,1,0:T(8,128)(2,1)}, u32[]{:S(2)}, u32[]{:S(2)}) async-start(bf16[128,1,32,512]{3,2,1,0:T(8,128)(2,1)} %bitcast.55), calls=%async_computation.1 | async-start | bytes 8388608 | tf_op jit(solution)/shard_map/all_to_all | solution.py:23
  50.9 0.1 reshape_squeeze.9
  51.0 7.4 %copy.37 = bf16[128,8,24,128]{3,2,1,0:T(8,128)(2,1)} copy(bf16[128,8,24,128]{3,1,2,0:T(8,128)(2,1)} %bitcast.56) | data formatting | bytes 12582912
  58.5 95.6 %all-to-all-done.1 = bf16[128,1,32,512]{3,2,1,0:T(8,128)(2,1)} async-done(((bf16[128,1,32,512]{3,2,1,0:T(8,128)(2,1)}), bf16[128,1,32,512]{3,2,1,0:T(8,128)(2,1)}, u32[]{:S(2)}, u32[]{:S(2)}) %all-to-all-start.1) | async-done | bytes 4194336 | tf_op jit(solution)/shard_map/all_to_all | solution.py:23
  154.1 2.8 gather_fusion.1
  156.9 0.0 copy-start
  156.9 97.7 %all-gather.2.cloned.1.call-done = bf16[2,512,3072]{1,2,0:T(8,128)(2,1)} async-done(((bf16[2,512,24]{1,2,0:T(8,128)(2,1)}), bf16[2,512,3072]{1,2,0:T(8,128)(2,1)}) %all-gather.2.cloned.1.call-update) | async-done | bytes 6291472 | tf_op jit(solution)/shard_map/all_gather | solution.py:40
  254.6 0.0 copy-done
  254.6 5.6 %convert_bitcast_fusion.2 = bf16[128,8,24,128]{3,1,2,0:T(8,128)(2,1)S(1)} fusion(bf16[1024,512]{1,0:T(8,128)(2,1)S(1)} %bitcast.58, bf16[2,512,3072]{1,2,0:T(8,128)(2,1)} %all-gather.2.cloned.1.call-done), kind=kOutput, calls=%fused_computation.18 | convolution fusion | flops 3224371200 | bytes 10485760 | tf_op jit(solution)/shard_map/dot_general | solution.py:42
  260.2 0.0 copy-start.1
  260.2 0.0 slice-start
  260.2 4.7 %copy.35 = bf16[128,8,24,128]{3,2,1,0:T(8,128)(2,1)} copy(bf16[128,8,24,128]{3,1,2,0:T(8,128)(2,1)S(1)} %convert_bitcast_fusion.2) | data formatting | bytes 12582912
  264.8 0.0 copy-done.1
  264.8 0.0 slice-start.1
  264.8 5.9 %convert_bitcast_fusion.1 = bf16[128,8,24,128]{3,1,2,0:T(8,128)(2,1)S(1)} fusion(bf16[1024,512]{1,0:T(8,128)(2,1)S(1)} %bitcast.59, bf16[2,512,3072]{1,2,0:T(8,128)(2,1)} %all-gather.2.cloned.1.call-done), kind=kOutput, calls=%fused_computation.17 | convolution fusion | flops 3224371200 | bytes 10485760 | tf_op jit(solution)/shard_map/dot_general | solution.py:41
  270.8 4.6 %copy.36 = bf16[128,8,24,128]{3,2,1,0:T(8,128)(2,1)} copy(bf16[128,8,24,128]{3,1,2,0:T(8,128)(2,1)S(1)} %convert_bitcast_fusion.1) | data formatting | bytes 12582912
  275.3 0.0 slice-done
  275.4 0.0 slice-done.1
  275.4 10.8 %fusion.8 = f32[16,24,64,64]{3,2,1,0:T(8,128)} fusion(bf16[16,64,24,128]{3,2,1,0:T(8,128)(2,1)S(1)} %bitcast.53, bf16[16,64,24,128]{3,2,1,0:T(8,128)(2,1)} %bitcast.54), kind=kOutput, calls=%fused_computation.11 | convolution fusion | flops 402653184 | bytes 18874368 | tf_op jit(solution)/shard_map/cthd,cuhd->chtu/dot_general | solution.py:49
  286.1 16.3 %fusion.19 = (f32[16,24,64]{2,1,0:T(8,128)S(1)}, f32[16,24,64,64]{2,3,1,0:T(8,128)}) fusion(f32[16,24,64,64]{3,2,1,0:T(8,128)} %fusion.8), kind=kOutput, calls=%fused_computation.44 | output fusion | flops 6291519 | bytes 12681216 | tf_op jit(solution)/shard_map/sub | solution.py:52
  302.4 8.1 %convert_bitcast_fusion = bf16[16,64,24,128]{3,1,2,0:T(8,128)(2,1)S(1)} fusion(f32[16,24,64,64]{2,3,1,0:T(8,128)} %get-tuple-element.8, f32[16,24,64]{2,1,0:T(8,128)S(1)} %get-tuple-element.7, bf16[16,64,24,128]{3,2,1,0:T(8,128)(2,1)} %bitcast.57), kind=kOutput, calls=%fused_computation.14 | convolution fusion | flops 408944640 | bytes 18972672 | tf_op jit(solution)/shard_map/chtu,cuhd->cthd/dot_general | solution.py:53
  310.5 8.0 %copy.33 = bf16[16,64,24,128]{3,2,1,0:T(8,128)(2,1)} copy(bf16[16,64,24,128]{3,1,2,0:T(8,128)(2,1)S(1)} %convert_bitcast_fusion) | data formatting | bytes 12582912 | tf_op jit(solution)/shard_map/convert_element_type | solution.py:54
  318.5 10.3 %reshape.181 = bf16[1,16,64,3072]{3,2,1,0:T(8,128)(2,1)} reshape(bf16[16,64,24,128]{3,2,1,0:T(8,128)(2,1)} %copy.33) | data formatting | bytes 12582912 | tf_op jit(solution)/shard_map/reshape | solution.py:54
  (7 shorter events, 0.1 us)
Async XLA Ops:
  6.5 248.0 %all-gather.2.cloned.1.call-start = ((), (), s32[]{:S(2)}) async-start(), calls=%async_computation.2 | async-start | bytes 6340608 | tf_op jit(solution)/shard_map/all_gather | solution.py:40
  9.3 25.0 %all-to-all-start = ((s32[128,1,1]{2,1,0:T(1,128)}), s32[128,1,1]{2,1,0:T(1,128)S(1)}, u32[]{:S(2)}, u32[]{:S(2)}) async-start(s32[128,1,1]{2,1,0:T(1,128)} %copy.27), calls=%async_computation | async-start | bytes 131072 | tf_op jit(solution)/shard_map/all_to_all | solution.py:21
  24.1 12.6 %collective-permute-start = (bf16[8,32,512]{2,1,0:T(8,128)(2,1)}, bf16[8,32,512]{2,1,0:T(8,128)(2,1)S(1)}, u32[]{:S(2)}, u32[]{:S(2)}) collective-permute-start(bf16[8,32,512]{2,1,0:T(8,128)(2,1)} %bitcast.61), channel_id=1, source_target_pairs={{0,1},{1,0},{2,3},{3,2},{4,5},{5,4},{6,7},{7,6},{8,9},{9,8},{10,11... | collective-permute-start | bytes 786440 | tf_op jit(solution)/shard_map/ppermute | solution.py:10
  39.5 114.5 %all-to-all-start.1 = ((bf16[128,1,32,512]{3,2,1,0:T(8,128)(2,1)}), bf16[128,1,32,512]{3,2,1,0:T(8,128)(2,1)}, u32[]{:S(2)}, u32[]{:S(2)}) async-start(bf16[128,1,32,512]{3,2,1,0:T(8,128)(2,1)} %bitcast.55), calls=%async_computation.1 | async-start | bytes 8388608 | tf_op jit(solution)/shard_map/all_to_all | solution.py:23
  156.9 97.7 %copy-start = (bf16[32,32,512]{2,1,0:T(8,128)(2,1)}, bf16[32,32,512]{2,1,0:T(8,128)(2,1)S(1)}, u32[]{:S(2)}) copy-start(bf16[32,32,512]{2,1,0:T(8,128)(2,1)S(1)} %gather_fusion.1) | copy-start | bytes 3145732
  260.2 4.7 %copy-start.1 = (bf16[32,32,512]{2,1,0:T(8,128)(2,1)S(1)}, bf16[32,32,512]{2,1,0:T(8,128)(2,1)}, u32[]{:S(2)}) copy-start(bf16[32,32,512]{2,1,0:T(8,128)(2,1)} %copy-done) | copy-start | bytes 3145732
  260.2 15.2 %slice-start = ((s8[6291456]{0:T(1024)(128)(4,1)}), s8[4194304]{0:T(1024)(128)(4,1)S(1)}, s32[]{:S(2)}) async-start(s8[6291456]{0:T(1024)(128)(4,1)} %bitcast.51), calls=%async_computation.3 | async-start | bytes 8388608
  264.8 10.5 %slice-start.1 = ((s8[6291456]{0:T(1024)(128)(4,1)}), s8[2097152]{0:T(1024)(128)(4,1)S(1)}, s32[]{:S(2)}) async-start(s8[6291456]{0:T(1024)(128)(4,1)} %bitcast.51), calls=%async_computation.4 | async-start | bytes 4194304
Sparse Core Ops, SparseCore 0:
  9.2 245.3 all-gather.1
where the time goes:
time: 339 us; the launch traced here: 336 us
  waiting for transfers between devices  201 us (59%)
  local copies, waits for them, and re-layouts  42.3 us (12%)
  matrix products  30.4 us (9%)
  starting transfers between devices  28.9 us (9%)
  other arithmetic  19.1 us (6%)
  between operations  13.5 us (4%)
    all_gather x1, waiting for transfers between devices, body(): piece = lax.all_gather(kv_weight, 'seq', axis=2, tiled=True)  97.7 us
    all_to_all x1, waiting for transfers between devices, fetch_rows(): lax.all_to_all(rows, 'seq', split_axis=0, concat_axis=0, tiled=True)  95.6 us
    unnamed x12, local copies, waits for them, and re-layouts  17.4 us
    sub x1, other arithmetic, body(): probs = jax.nn.softmax(scores, axis=-1).astype(jnp.bfloat16)  16.3 us
    all_to_all x1, starting transfers between devices, fetch_rows(): lax.all_to_all(request, 'seq', split_axis=0, concat_axis=0, tiled=True)  14.8 us
    all_to_all x1, starting transfers between devices, fetch_rows(): lax.all_to_all(rows, 'seq', split_axis=0, concat_axis=0, tiled=True)  11.4 us
    dot_general x1, matrix products, body(): jnp.einsum('cthd,cuhd->chtu', query_block, keys, preferred_element_type=j...  10.8 us
    reshape x1, local copies, waits for them, and re-layouts, body(): mixed.astype(jnp.bfloat16)  10.3 us
  transfers between devices with their start and end apart: 4, of which 3 were waited for; matrix products, arithmetic and copies ran while one was open for 5% of the time, Pallas kernels for 0%

commit v1 on v0

v1 whole, which is shorter than its diff:
```python
import jax
import jax.numpy as jnp
from jax import lax
from jax.experimental import pallas as pl
from jax.experimental.pallas import tpu as pltpu
from jax.sharding import Mesh, PartitionSpec as P

HDIM = 128
NZ, NX, NY, NC = 8, 4, 2, 2
PLANE = NX * NY * NC
NEAR = (0, 1, NZ - 1)
FAR = tuple(range(2, NZ - 1))
PAIR = 2
STEPS = 4
BATCH = 16
SCALE = HDIM ** -0.5
MASKED = -1e30
CONTRACT = (((1,), (1,)), ((), ()))


def shift(count, step):
    return [(i, (i + step) % count) for i in range(count)]


def hop(below, above):
    moved = lax.ppermute(below, "z", shift(NZ, -1)), lax.ppermute(above, "z", shift(NZ, 1))
    return lax.optimization_barrier(moved)


def attend_kernel(near, index, place, q_ref, *refs):
    parts = NZ // STEPS
    own_refs, other_refs = refs[:parts], refs[parts:2 * parts]
    near_rows, far_rows, out_ref, rows, kv, sems = refs[2 * parts:]
    blocks = near.shape[0]
    tokens = rows.shape[0] // blocks
    features = own_refs[0].shape[1]

    def copy(j, source):
        return pltpu.make_async_copy(
            source.at[index[j]], rows.at[pl.ds(j * tokens, tokens)], sems.at[j]
        )

    @pl.when(pl.program_id(0) == 0)
    def _():
        for j in range(blocks):
            @pl.when(near[j] == 1)
            def _():
                copy(j, near_rows).start()

            @pl.when(near[j] == 0)
            def _():
                copy(j, far_rows).start()
        for j in range(blocks):
            copy(j, far_rows).wait()

    core = place[1]
    for part in range(parts):
        at = pl.ds(part * features, features)
        for kind, weight in ((core, own_refs[part]), (1 - core, other_refs[part])):
            kv[kind, :, at] = lax.dot_general(
                rows[...], weight[0], CONTRACT, preferred_element_type=jnp.float32
            ).astype(jnp.bfloat16)

    span = 2 * tokens
    size = PAIR * span
    row = lax.broadcasted_iota(jnp.int32, (size, size), 0) // span
    col = lax.broadcasted_iota(jnp.int32, (size, size), 1) // span
    same = row == col
    ones = jnp.ones((size, HDIM), jnp.bfloat16)
    tiles = [
        (pl.ds(group * size, size), pl.ds(head * HDIM, HDIM))
        for head in range(q_ref.shape[1] // HDIM)
        for group in range(rows.shape[0] // size)
    ]
    for first in range(0, len(tiles), BATCH):
        batch = tiles[first:first + BATCH]
        scores = [
            lax.dot_general(q_ref[tile], kv[(0,) + tile], CONTRACT, preferred_element_type=jnp.float32)
            for tile in batch
        ]
        weights = []
        for score in scores:
            score = jnp.where(same, score * SCALE, MASKED)
            weights.append(jnp.exp(score - jnp.max(score, axis=1, keepdims=True)).astype(jnp.bfloat16))
        for tile, weight in zip(batch, weights):
            both = jnp.concatenate([kv[(1,) + tile], ones], axis=1)
            mixed = jnp.dot(weight, both, preferred_element_type=jnp.float32)
            out_ref[tile] = (mixed[:, :HDIM] / mixed[:, HDIM:]).astype(jnp.bfloat16)


def attend(near, index, place, queries, own, other, near_rows, far_rows):
    tokens, features = queries.shape
    wide = features // STEPS
    parts = NZ // STEPS
    rows = near.shape[0] * near_rows.shape[1]
    width = near_rows.shape[2]
    weight_specs = [
        pl.BlockSpec(
            (1, features // NZ, width),
            lambda g, near, index, place, part=part: ((g * parts + part - place[0]) % NZ, 0, 0),
        )
        for part in range(parts)
    ]
    block = pl.BlockSpec((tokens, wide), lambda g, near, index, place: (0, g))
    whole = pl.BlockSpec(memory_space=pl.ANY)
    return pl.pallas_call(
        attend_kernel,
        out_shape=jax.ShapeDtypeStruct((tokens, features), jnp.bfloat16),
        grid_spec=pltpu.PrefetchScalarGridSpec(
            num_scalar_prefetch=3,
            grid=(STEPS,),
            in_specs=[block] + weight_specs * 2 + [whole, whole],
            out_specs=block,
            scratch_shapes=[
                pltpu.VMEM((rows, width), jnp.bfloat16),
                pltpu.VMEM((2, rows, wide), jnp.bfloat16),
                pltpu.SemaphoreType.DMA((near.shape[0],)),
            ],
        ),
        compiler_params=pltpu.CompilerParams(
            dimension_semantics=("arbitrary",), vmem_limit_bytes=48 << 20
        ),
        cost_estimate=pl.CostEstimate(
            flops=4 * rows * width * features + 8 * tokens * HDIM * features,
            bytes_accessed=4 * tokens * features + 4 * width * features,
            transcendentals=tokens * 128 * features // HDIM,
        ),
    )(near, index, place, queries, *[own] * parts, *[other] * parts, near_rows, far_rows)


def select(pieces, asked, at):
    wanted = jnp.stack([asked[:, ahead] for ahead in at], axis=1)
    wanted = wanted + jnp.arange(len(at))[None, :] * pieces[0].shape[0]
    return jnp.concatenate(pieces)[wanted.reshape(-1)]


def exchange(parcels):
    return lax.all_to_all(parcels, ("x", "y", "c"), split_axis=0, concat_axis=0, tiled=True)


def body(queries, encoded, neighbours, kv_weight):
    plane = ("x", "y", "c")
    blocks_each = encoded.shape[1]
    width = encoded.shape[3]
    z = lax.axis_index("z")
    core = lax.axis_index("c")

    block_ids = neighbours[0].reshape(-1)
    owner = block_ids // blocks_each
    local = block_ids % blocks_each
    column = owner % PLANE
    ahead = (owner // PLANE - z) % NZ
    placed = (column * NZ + ahead)[:, None] == jnp.arange(PLANE * NZ)[None, :]
    request = jnp.sum(jnp.where(placed, local[:, None], 0), 0).reshape(PLANE, NZ)
    near = (ahead < 2) | (ahead == NZ - 1)
    index = jnp.where(
        near, column * len(NEAR) + jnp.minimum(ahead, 2), column * len(FAR) + ahead - 2
    )

    shard = kv_weight.transpose(0, 2, 1)
    columns = shard.shape[1]
    shards = jnp.broadcast_to(shard, (NX * NY,) + shard.shape).reshape((PLANE,) + shard.shape[1:])
    letter = jnp.pad(request.astype(jnp.bfloat16)[:, None, :], ((0, 0), (0, 7), (0, width - NZ)))
    parcel = jnp.concatenate([shards, letter], axis=1)

    here = lax.ppermute(encoded[0], "sec", shift(2, 1))
    here, parcel = lax.optimization_barrier((here, parcel))
    parcel = exchange(parcel)
    asked = parcel[:, columns, :NZ].astype(jnp.int32)
    piece = parcel[:, :columns].reshape(-1, width)
    below1, above1 = hop(here, here)
    near_rows = select([here, below1, above1], asked, NEAR)
    below1, above1, near_rows = lax.optimization_barrier((below1, above1, near_rows))
    near_rows = exchange(near_rows)
    below2, above2 = hop(below1, above1)
    below3, above3 = hop(below2, above2)
    below4 = lax.ppermute(below3, "z", shift(NZ, -1))
    far_rows = select([below2, below3, below4, above3, above2], asked, FAR)
    far_rows, near_rows, piece = lax.optimization_barrier((far_rows, near_rows, piece))
    far_rows = exchange(far_rows)

    w1, v1 = hop(piece, piece)
    w2, v2 = hop(w1, v1)
    w3, v3 = hop(w2, v2)
    w4 = lax.ppermute(w3, "z", shift(NZ, -1))
    pieces = [piece, w1, w2, w3, w4, v3, v2, v1]
    own = jnp.stack(pieces)
    other = jnp.stack([lax.ppermute(part, "c", shift(2, 1)) for part in pieces])

    place = jnp.stack([z, core])
    flat = queries.reshape(-1, queries.shape[3])
    out = attend(near.astype(jnp.int32), index, place, flat, own, other, near_rows, far_rows)
    return out.reshape(queries.shape)


def solution(mesh):
    fine = Mesh(mesh.devices.reshape(NZ, NX, NY, NC, 2), ("z", "x", "y", "c", "sec"))
    seq = ("z", "x", "y", "c")
    placed = (
        P("sec", seq, None, None),
        P("sec", seq, None, None),
        P("sec", seq, None),
        P(None, None, seq),
    )
    return jax.shard_map(
        body, mesh=fine, in_specs=placed, out_specs=P("sec", seq, None, None), check_vma=False
    )
```

time: 339 us -> 152 us (0.45)
  waiting for transfers between devices: 201 us -> 55.3 us
  matrix products: 30.4 us -> 0 us
  Pallas kernels: 0 us -> 24 us
  local copies, waits for them, and re-layouts: 42.3 us -> 21.7 us
  starting transfers between devices: 28.9 us -> 48.5 us
  other arithmetic: 19.1 us -> 1.34 us
  between operations: 13.5 us -> 0.4 us
    all_to_all x2 -> x3, waiting for transfers between devices: 103 us -> 0.01 us  [exchange(): lax.all_to_all(parcels, ('x', 'y', 'c'), split_axis=0, concat_axis=0, til...]
    all_gather x1 -> x0, waiting for transfers between devices: 97.7 us -> none  [body(): piece = lax.all_gather(kv_weight, 'seq', axis=2, tiled=True)]
    ppermute x1 -> x23, waiting for transfers between devices: 0.01 us -> 55.3 us  [the longest x6 24.2 us: hop(): lax.ppermute(below, 'z', shift(NZ, -1))]
    dot_general x4 -> x0, matrix products: 30.4 us -> none  [the longest x1 10.8 us: body(): jnp.einsum('cthd,cuhd->chtu', query_block, keys, preferred_element_type=j...]
    ppermute x1 -> x23, starting transfers between devices: 2.71 us -> 29.8 us  [the longest x6 12.6 us: hop(): lax.ppermute(below, 'z', shift(NZ, -1))]
    pallas_call x0 -> x1, Pallas kernels: none -> 24 us  [attend(): pl.pallas_call(attend_kernel, out_shape=jax.ShapeDtypeStruct((tokens, fea...]
    sub x1 -> x0, other arithmetic: 16.3 us -> none  [body(): probs = jax.nn.softmax(scores, axis=-1).astype(jnp.bfloat16)]
    reshape x1 -> x0, local copies, waits for them, and re-layouts: 10.3 us -> none  [body(): mixed.astype(jnp.bfloat16)]
  transfers between devices with their start and end apart: 4 -> 26, of which waited for: 3 -> 12; matrix products, arithmetic and copies ran while one was open for 5% -> 12% of each run, Pallas kernels for 0% -> 0%
where the time goes in v1:
time: 152 us; the launch traced here: 151 us
  waiting for transfers between devices  55.3 us (36%)
  starting transfers between devices  48.5 us (32%)
  Pallas kernels  24 us (16%)
  local copies, waits for them, and re-layouts  21.7 us (14%)
    ppermute x6, waiting for transfers between devices, hop(): lax.ppermute(below, 'z', shift(NZ, -1))  24.2 us
    pallas_call x1, Pallas kernels, attend(): pl.pallas_call(attend_kernel, out_shape=jax.ShapeDtypeStruct((tokens, fea...  24 us
    all_to_all x3, starting transfers between devices, exchange(): lax.all_to_all(parcels, ('x', 'y', 'c'), split_axis=0, concat_axis=0, til...  18.7 us
    ppermute x6, waiting for transfers between devices, hop(): lax.ppermute(above, 'z', shift(NZ, 1))  15.6 us
    unnamed x26, local copies, waits for them, and re-layouts  14.2 us
    ppermute x6, starting transfers between devices, hop(): lax.ppermute(below, 'z', shift(NZ, -1))  12.6 us
    ppermute x1, waiting for transfers between devices, body(): w4 = lax.ppermute(w3, 'z', shift(NZ, -1))  9.55 us
    ppermute x8, starting transfers between devices, body(): other = jnp.stack([lax.ppermute(part, 'c', shift(2, 1)) for part in pieces])  8.87 us
  transfers between devices with their start and end apart: 26, of which 12 were waited for; matrix products, arithmetic and copies ran while one was open for 12% of the time, Pallas kernels for 0%

profile of v1, /device:TPU:1, one launch (start us, length us, event | category | flops | bytes accessed | tf_op | source)
XLA Modules:
  0.0 151.2 jit_solution(3068011546027173026)
XLA Ops:
  0.0 3.7 %collective-permute-start = (bf16[8,32,512]{2,1,0:T(8,128)(2,1)}, bf16[8,32,512]{2,1,0:T(8,128)(2,1)S(1)}, u32[]{:S(2)}, u32[]{:S(2)}) collective-permute-start(bf16[8,32,512]{2,1,0:T(8,128)(2,1)} %bitcast.54), channel_id=1, source_target_pairs={{0,1},{1,0},{2,3},{3,2},{4,5},{5,4},{6,7},{7,6},{8,9},{9,8},{10,11... | collective-permute-start | bytes 786440 | tf_op jit(solution)/shard_map/ppermute | solution.py:166
  3.7 0.8 copy.27
  4.5 0.1 reshape_squeeze.3
  4.6 0.1 select_reduce_fusion
  4.7 0.1 convert_element_type.30
  4.8 0.8 broadcast_in_dim.14
  5.7 0.9 fusion.1
  6.5 2.5 %collective-permute-done = bf16[8,32,512]{2,1,0:T(8,128)(2,1)S(1)} collective-permute-done((bf16[8,32,512]{2,1,0:T(8,128)(2,1)}, bf16[8,32,512]{2,1,0:T(8,128)(2,1)S(1)}, u32[]{:S(2)}, u32[]{:S(2)}) %collective-permute-start) | collective-permute-done | bytes 262176 | tf_op jit(solution)/shard_map/ppermute | solution.py:166
  9.0 7.6 %all-to-all-start = ((bf16[16,32,512]{2,1,0:T(8,128)(2,1)}), bf16[16,32,512]{2,1,0:T(8,128)(2,1)S(1)}, u32[]{:S(2)}, u32[]{:S(2)}) async-start(bf16[16,32,512]{2,1,0:T(8,128)(2,1)} %fusion.1), calls=%async_computation | async-start | bytes 1048576 | tf_op jit(solution)/shard_map/all_to_all | solution.py:138
  16.6 1.6 %collective-permute-start.2 = (bf16[8,32,512]{2,1,0:T(8,128)(2,1)S(1)}, bf16[8,32,512]{2,1,0:T(8,128)(2,1)S(1)}, u32[]{:S(2)}, u32[]{:S(2)}) collective-permute-start(bf16[8,32,512]{2,1,0:T(8,128)(2,1)S(1)} %collective-permute-done), channel_id=1, source_target_pairs={{0,32},{32,64},{64,96},{96,128},{128,160},{160,192},{192,224},{224... | collective-permute-start | bytes 786440 | tf_op jit(solution)/shard_map/ppermute | solution.py:26
  18.2 4.0 %collective-permute-start.1 = (bf16[8,32,512]{2,1,0:T(8,128)(2,1)S(1)}, bf16[8,32,512]{2,1,0:T(8,128)(2,1)S(1)}, u32[]{:S(2)}, u32[]{:S(2)}) collective-permute-start(bf16[8,32,512]{2,1,0:T(8,128)(2,1)S(1)} %collective-permute-done), channel_id=1, source_target_pairs={{0,224},{32,0},{64,32},{96,64},{128,96},{160,128},{192,160},{224,1... | collective-permute-start | bytes 786440 | tf_op jit(solution)/shard_map/ppermute | solution.py:26
  22.3 6.5 %collective-permute-done.2 = bf16[8,32,512]{2,1,0:T(8,128)(2,1)S(1)} collective-permute-done((bf16[8,32,512]{2,1,0:T(8,128)(2,1)S(1)}, bf16[8,32,512]{2,1,0:T(8,128)(2,1)S(1)}, u32[]{:S(2)}, u32[]{:S(2)}) %collective-permute-start.2) | collective-permute-done | bytes 262176 | tf_op jit(solution)/shard_map/ppermute | solution.py:26
  28.8 0.1 pad_maximum_fusion
  28.9 0.1 copy.32
  29.1 0.1 copy.30
  29.1 0.1 add.124
  29.3 1.9 %gather_fusion = bf16[48,32,512]{2,1,0:T(8,128)(2,1)} fusion(bf16[24,32,512]{2,1,0:T(8,128)(2,1)S(1)} %pad_maximum_fusion, s32[1024]{0:T(1024)S(1)} %pad_clamp_fusion.1), kind=kCustom, calls=%fused_computation | custom fusion | bytes 3145920 | tf_op jit(solution)/shard_map/gather | solution.py:134
  31.2 6.0 %all-to-all-start.1 = ((bf16[48,32,512]{2,1,0:T(8,128)(2,1)}), bf16[48,32,512]{2,1,0:T(8,128)(2,1)S(1)}, u32[]{:S(2)}, u32[]{:S(2)}) async-start(bf16[48,32,512]{2,1,0:T(8,128)(2,1)} %gather_fusion), calls=%async_computation.1 | async-start | bytes 3145728 | tf_op jit(solution)/shard_map/all_to_all | solution.py:138
  37.2 2.8 %collective-permute-start.3 = (bf16[8,32,512]{2,1,0:T(8,128)(2,1)S(1)}, bf16[8,32,512]{2,1,0:T(8,128)(2,1)}, u32[]{:S(2)}, u32[]{:S(2)}) collective-permute-start(bf16[8,32,512]{2,1,0:T(8,128)(2,1)S(1)} %collective-permute-done.1), channel_id=1, source_target_pairs={{0,224},{32,0},{64,32},{96,64},{128,96},{160,128},{192,160},{224,1... | collective-permute-start | bytes 786440 | tf_op jit(solution)/shard_map/ppermute | solution.py:26
  40.0 5.5 %collective-permute-done.3 = bf16[8,32,512]{2,1,0:T(8,128)(2,1)} collective-permute-done((bf16[8,32,512]{2,1,0:T(8,128)(2,1)S(1)}, bf16[8,32,512]{2,1,0:T(8,128)(2,1)}, u32[]{:S(2)}, u32[]{:S(2)}) %collective-permute-start.3) | collective-permute-done | bytes 262176 | tf_op jit(solution)/shard_map/ppermute | solution.py:26
  45.5 3.1 %collective-permute-done.4 = bf16[8,32,512]{2,1,0:T(8,128)(2,1)S(1)} collective-permute-done((bf16[8,32,512]{2,1,0:T(8,128)(2,1)S(1)}, bf16[8,32,512]{2,1,0:T(8,128)(2,1)S(1)}, u32[]{:S(2)}, u32[]{:S(2)}) %collective-permute-start.4) | collective-permute-done | bytes 262176 | tf_op jit(solution)/shard_map/ppermute | solution.py:26
  48.6 0.4 collective-permute-start.5
  49.0 1.0 collective-permute-start.6
  50.1 0.1 copy.31
  50.2 0.1 add.129
  50.3 5.1 %collective-permute-done.5 = bf16[8,32,512]{2,1,0:T(8,128)(2,1)} collective-permute-done((bf16[8,32,512]{2,1,0:T(8,128)(2,1)}, bf16[8,32,512]{2,1,0:T(8,128)(2,1)}, u32[]{:S(2)}, u32[]{:S(2)}) %collective-permute-start.5) | collective-permute-done | bytes 262176 | tf_op jit(solution)/shard_map/ppermute | solution.py:26
  55.4 1.5 collective-permute-done.6
  56.9 0.5 collective-permute-start.7
  57.4 1.0 constant_dynamic-update-slice_fusion.4
  58.4 1.0 constant_dynamic-update-slice_fusion.3
  59.4 3.3 %collective-permute-done.7 = bf16[8,32,512]{2,1,0:T(8,128)(2,1)S(1)} collective-permute-done((bf16[8,32,512]{2,1,0:T(8,128)(2,1)}, bf16[8,32,512]{2,1,0:T(8,128)(2,1)S(1)}, u32[]{:S(2)}, u32[]{:S(2)}) %collective-permute-start.7) | collective-permute-done | bytes 262176 | tf_op jit(solution)/shard_map/ppermute | solution.py:177
  62.7 1.0 constant_dynamic-update-slice_fusion.1
  63.7 2.4 %gather_fusion.1 = bf16[80,32,512]{2,1,0:T(8,128)(2,1)} fusion(bf16[40,32,512]{2,1,0:T(8,128)(2,1)S(1)} %constant_dynamic-update-slice_fusion, s32[1024]{0:T(1024)S(1)} %pad_clamp_fusion), kind=kCustom, calls=%fused_computation.1 | custom fusion | bytes 5243200 | tf_op jit(solution)/shard_map/gather | solution.py:134
  66.1 1.1 copy-done
  67.3 2.7 %collective-permute-start.8 = (bf16[384,512]{1,0:T(8,128)(2,1)S(1)}, bf16[384,512]{1,0:T(8,128)(2,1)}, u32[]{:S(2)}, u32[]{:S(2)}) collective-permute-start(bf16[384,512]{1,0:T(8,128)(2,1)S(1)} %bitcast.48), channel_id=1, source_target_pairs={{0,224},{32,0},{64,32},{96,64},{128,96},{160,128},{192,160},{224,1... | collective-permute-start | bytes 1179656 | tf_op jit(solution)/shard_map/ppermute | solution.py:26
  70.0 0.1 pad_add_fusion.place
  70.0 3.7 %collective-permute-start.15 = (bf16[384,512]{1,0:T(8,128)(2,1)S(1)}, bf16[384,512]{1,0:T(8,128)(2,1)}, u32[]{:S(2)}, u32[]{:S(2)}) collective-permute-start(bf16[384,512]{1,0:T(8,128)(2,1)S(1)} %bitcast.49), channel_id=1, source_target_pairs={{0,2},{2,0},{1,3},{3,1},{4,6},{6,4},{5,7},{7,5},{8,10},{10,8},{9,1... | collective-permute-start | bytes 1179656 | tf_op jit(solution)/shard_map/ppermute | solution.py:188
  73.7 5.1 %all-to-all-start.2 = ((bf16[80,32,512]{2,1,0:T(8,128)(2,1)}), bf16[80,32,512]{2,1,0:T(8,128)(2,1)S(1)}, u32[]{:S(2)}, u32[]{:S(2)}) async-start(bf16[80,32,512]{2,1,0:T(8,128)(2,1)} %gather_fusion.1), calls=%async_computation.2 | async-start | bytes 5242880 | tf_op jit(solution)/shard_map/all_to_all | solution.py:138
  78.9 1.3 collective-permute-start.16
  80.1 2.7 %collective-permute-start.10 = (bf16[384,512]{1,0:T(8,128)(2,1)}, bf16[384,512]{1,0:T(8,128)(2,1)S(1)}, u32[]{:S(2)}, u32[]{:S(2)}) collective-permute-start(bf16[384,512]{1,0:T(8,128)(2,1)} %collective-permute-done.8), channel_id=1, source_target_pairs={{0,224},{32,0},{64,32},{96,64},{128,96},{160,128},{192,160},{224,1... | collective-permute-start | bytes 1179656 | tf_op jit(solution)/shard_map/ppermute | solution.py:26
  82.8 0.3 collective-permute-start.22
  83.1 1.0 bitcast_dynamic-update-slice_fusion.14
  84.1 1.8 %bitcast_dynamic-update-slice_fusion.7 = bf16[8,384,512]{2,1,0:T(8,128)(2,1)} fusion(bf16[384,512]{1,0:T(8,128)(2,1)} %collective-permute-done.15), kind=kLoop, calls=%fused_computation.13 | loop fusion | bytes 786432
  85.9 5.8 %collective-permute-done.10 = bf16[384,512]{1,0:T(8,128)(2,1)S(1)} collective-permute-done((bf16[384,512]{1,0:T(8,128)(2,1)}, bf16[384,512]{1,0:T(8,128)(2,1)S(1)}, u32[]{:S(2)}, u32[]{:S(2)}) %collective-permute-start.10) | collective-permute-done | bytes 393248 | tf_op jit(solution)/shard_map/ppermute | solution.py:26
  91.7 3.3 %collective-permute-done.11 = bf16[384,512]{1,0:T(8,128)(2,1)S(1)} collective-permute-done((bf16[384,512]{1,0:T(8,128)(2,1)}, bf16[384,512]{1,0:T(8,128)(2,1)S(1)}, u32[]{:S(2)}, u32[]{:S(2)}) %collective-permute-start.11) | collective-permute-done | bytes 393248 | tf_op jit(solution)/shard_map/ppermute | solution.py:26
  95.0 1.0 collective-permute-start.17
  96.0 1.5 collective-permute-start.13
  97.5 0.7 collective-permute-start.21
  98.2 0.8 bitcast_dynamic-update-slice_fusion.6
  99.0 7.8 %collective-permute-done.12 = bf16[384,512]{1,0:T(8,128)(2,1)S(1)} collective-permute-done((bf16[384,512]{1,0:T(8,128)(2,1)S(1)}, bf16[384,512]{1,0:T(8,128)(2,1)S(1)}, u32[]{:S(2)}, u32[]{:S(2)}) %collective-permute-start.12) | collective-permute-done | bytes 393248 | tf_op jit(solution)/shard_map/ppermute | solution.py:26
  106.8 1.2 collective-permute-done.13
  108.0 0.8 collective-permute-start.18
  108.8 0.4 collective-permute-start.20
  109.2 0.8 bitcast_dynamic-update-slice_fusion.5
  110.0 9.6 %collective-permute-done.14 = bf16[384,512]{1,0:T(8,128)(2,1)S(1)} collective-permute-done((bf16[384,512]{1,0:T(8,128)(2,1)S(1)}, bf16[384,512]{1,0:T(8,128)(2,1)S(1)}, u32[]{:S(2)}, u32[]{:S(2)}) %collective-permute-start.14) | collective-permute-done | bytes 393248 | tf_op jit(solution)/shard_map/ppermute | solution.py:185
  119.5 0.8 collective-permute-start.19
  120.4 1.0 bitcast_dynamic-update-slice_fusion.8.refs_0_.refs_1_
  121.5 0.8 bitcast_dynamic-update-slice_fusion.4
  122.3 1.0 bitcast_dynamic-update-slice_fusion.3
  123.3 0.8 bitcast_dynamic-update-slice_fusion.2
  124.1 0.8 bitcast_dynamic-update-slice_fusion.1
  124.9 0.8 bitcast_dynamic-update-slice_fusion.refs_2_.refs_3_
  125.6 1.4 copy-done.1
  127.1 24.0 %shard_map.46 = bf16[1024,3072]{1,0:T(8,128)(2,1)} custom-call(s32[32]{0:T(128)S(1)} %fusion.5.near, s32[32]{0:T(128)S(1)} %add_select_fusion.index, s32[2]{0:T(128)S(1)} %pad_add_fusion.place, bf16[1024,3072]{1,0:T(8,128)(2,1)} %bitcast.53, bf16[8,384,512]{2,1,0:T(8,128)(2,1)} %copy-done.2, bf16[8,384,512]{2,1,0:T(8,128)(2,1)} %copy-done.2, ...), custom_call_target="tpu_custom_call" | custom-call | flops 9663676416 | bytes 18874368 | tf_op jit(solution)/shard_map/pallas_call | solution.py:106
  (49 shorter events, 0.5 us)
Async XLA Ops:
  0.0 9.0 %collective-permute-start = (bf16[8,32,512]{2,1,0:T(8,128)(2,1)}, bf16[8,32,512]{2,1,0:T(8,128)(2,1)S(1)}, u32[]{:S(2)}, u32[]{:S(2)}) collective-permute-start(bf16[8,32,512]{2,1,0:T(8,128)(2,1)} %bitcast.54), channel_id=1, source_target_pairs={{0,1},{1,0},{2,3},{3,2},{4,5},{5,4},{6,7},{7,6},{8,9},{9,8},{10,11... | collective-permute-start | bytes 786440 | tf_op jit(solution)/shard_map/ppermute | solution.py:166
  9.0 19.8 %all-to-all-start = ((bf16[16,32,512]{2,1,0:T(8,128)(2,1)}), bf16[16,32,512]{2,1,0:T(8,128)(2,1)S(1)}, u32[]{:S(2)}, u32[]{:S(2)}) async-start(bf16[16,32,512]{2,1,0:T(8,128)(2,1)} %fusion.1), calls=%async_computation | async-start | bytes 1048576 | tf_op jit(solution)/shard_map/all_to_all | solution.py:138
  16.6 12.2 %collective-permute-start.2 = (bf16[8,32,512]{2,1,0:T(8,128)(2,1)S(1)}, bf16[8,32,512]{2,1,0:T(8,128)(2,1)S(1)}, u32[]{:S(2)}, u32[]{:S(2)}) collective-permute-start(bf16[8,32,512]{2,1,0:T(8,128)(2,1)S(1)} %collective-permute-done), channel_id=1, source_target_pairs={{0,32},{32,64},{64,96},{96,128},{128,160},{160,192},{192,224},{224... | collective-permute-start | bytes 786440 | tf_op jit(solution)/shard_map/ppermute | solution.py:26
  18.2 10.5 %collective-permute-start.1 = (bf16[8,32,512]{2,1,0:T(8,128)(2,1)S(1)}, bf16[8,32,512]{2,1,0:T(8,128)(2,1)S(1)}, u32[]{:S(2)}, u32[]{:S(2)}) collective-permute-start(bf16[8,32,512]{2,1,0:T(8,128)(2,1)S(1)} %collective-permute-done), channel_id=1, source_target_pairs={{0,224},{32,0},{64,32},{96,64},{128,96},{160,128},{192,160},{224,1... | collective-permute-start | bytes 786440 | tf_op jit(solution)/shard_map/ppermute | solution.py:26
  31.2 35.0 %all-to-all-start.1 = ((bf16[48,32,512]{2,1,0:T(8,128)(2,1)}), bf16[48,32,512]{2,1,0:T(8,128)(2,1)S(1)}, u32[]{:S(2)}, u32[]{:S(2)}) async-start(bf16[48,32,512]{2,1,0:T(8,128)(2,1)} %gather_fusion), calls=%async_computation.1 | async-start | bytes 3145728 | tf_op jit(solution)/shard_map/all_to_all | solution.py:138
  37.2 8.3 %collective-permute-start.3 = (bf16[8,32,512]{2,1,0:T(8,128)(2,1)S(1)}, bf16[8,32,512]{2,1,0:T(8,128)(2,1)}, u32[]{:S(2)}, u32[]{:S(2)}) collective-permute-start(bf16[8,32,512]{2,1,0:T(8,128)(2,1)S(1)} %collective-permute-done.1), channel_id=1, source_target_pairs={{0,224},{32,0},{64,32},{96,64},{128,96},{160,128},{192,160},{224,1... | collective-permute-start | bytes 786440 | tf_op jit(solution)/shard_map/ppermute | solution.py:26
  40.0 8.6 %collective-permute-start.4 = (bf16[8,32,512]{2,1,0:T(8,128)(2,1)S(1)}, bf16[8,32,512]{2,1,0:T(8,128)(2,1)S(1)}, u32[]{:S(2)}, u32[]{:S(2)}) collective-permute-start(bf16[8,32,512]{2,1,0:T(8,128)(2,1)S(1)} %collective-permute-done.2), channel_id=1, source_target_pairs={{0,32},{32,64},{64,96},{96,128},{128,160},{160,192},{192,224},{224... | collective-permute-start | bytes 786440 | tf_op jit(solution)/shard_map/ppermute | solution.py:26
  48.6 6.8 %collective-permute-start.5 = (bf16[8,32,512]{2,1,0:T(8,128)(2,1)}, bf16[8,32,512]{2,1,0:T(8,128)(2,1)}, u32[]{:S(2)}, u32[]{:S(2)}) collective-permute-start(bf16[8,32,512]{2,1,0:T(8,128)(2,1)} %collective-permute-done.3), channel_id=1, source_target_pairs={{0,224},{32,0},{64,32},{96,64},{128,96},{160,128},{192,160},{224,1... | collective-permute-start | bytes 786440 | tf_op jit(solution)/shard_map/ppermute | solution.py:26
  49.0 7.9 %collective-permute-start.6 = (bf16[8,32,512]{2,1,0:T(8,128)(2,1)S(1)}, bf16[8,32,512]{2,1,0:T(8,128)(2,1)}, u32[]{:S(2)}, u32[]{:S(2)}) collective-permute-start(bf16[8,32,512]{2,1,0:T(8,128)(2,1)S(1)} %collective-permute-done.4), channel_id=1, source_target_pairs={{0,32},{32,64},{64,96},{96,128},{128,160},{160,192},{192,224},{224... | collective-permute-start | bytes 786440 | tf_op jit(solution)/shard_map/ppermute | solution.py:26
  56.9 5.8 %collective-permute-start.7 = (bf16[8,32,512]{2,1,0:T(8,128)(2,1)}, bf16[8,32,512]{2,1,0:T(8,128)(2,1)S(1)}, u32[]{:S(2)}, u32[]{:S(2)}) collective-permute-start(bf16[8,32,512]{2,1,0:T(8,128)(2,1)} %collective-permute-done.5), channel_id=1, source_target_pairs={{0,224},{32,0},{64,32},{96,64},{128,96},{160,128},{192,160},{224,1... | collective-permute-start | bytes 786440 | tf_op jit(solution)/shard_map/ppermute | solution.py:177
  66.1 1.1 copy-start
  67.3 11.6 %collective-permute-start.9 = (bf16[384,512]{1,0:T(8,128)(2,1)S(1)}, bf16[384,512]{1,0:T(8,128)(2,1)}, u32[]{:S(2)}, u32[]{:S(2)}) collective-permute-start(bf16[384,512]{1,0:T(8,128)(2,1)S(1)} %bitcast.47), channel_id=1, source_target_pairs={{0,32},{32,64},{64,96},{96,128},{128,160},{160,192},{192,224},{224... | collective-permute-start | bytes 1179656 | tf_op jit(solution)/shard_map/ppermute | solution.py:26
  67.3 11.6 %collective-permute-start.8 = (bf16[384,512]{1,0:T(8,128)(2,1)S(1)}, bf16[384,512]{1,0:T(8,128)(2,1)}, u32[]{:S(2)}, u32[]{:S(2)}) collective-permute-start(bf16[384,512]{1,0:T(8,128)(2,1)S(1)} %bitcast.48), channel_id=1, source_target_pairs={{0,224},{32,0},{64,32},{96,64},{128,96},{160,128},{192,160},{224,1... | collective-permute-start | bytes 1179656 | tf_op jit(solution)/shard_map/ppermute | solution.py:26
  70.0 14.1 %collective-permute-start.15 = (bf16[384,512]{1,0:T(8,128)(2,1)S(1)}, bf16[384,512]{1,0:T(8,128)(2,1)}, u32[]{:S(2)}, u32[]{:S(2)}) collective-permute-start(bf16[384,512]{1,0:T(8,128)(2,1)S(1)} %bitcast.49), channel_id=1, source_target_pairs={{0,2},{2,0},{1,3},{3,1},{4,6},{6,4},{5,7},{7,5},{8,10},{10,8},{9,1... | collective-permute-start | bytes 1179656 | tf_op jit(solution)/shard_map/ppermute | solution.py:188
  73.7 51.9 %all-to-all-start.2 = ((bf16[80,32,512]{2,1,0:T(8,128)(2,1)}), bf16[80,32,512]{2,1,0:T(8,128)(2,1)S(1)}, u32[]{:S(2)}, u32[]{:S(2)}) async-start(bf16[80,32,512]{2,1,0:T(8,128)(2,1)} %gather_fusion.1), calls=%async_computation.2 | async-start | bytes 5242880 | tf_op jit(solution)/shard_map/all_to_all | solution.py:138
  78.9 18.7 %collective-permute-start.16 = (bf16[384,512]{1,0:T(8,128)(2,1)}, bf16[384,512]{1,0:T(8,128)(2,1)S(1)}, u32[]{:S(2)}, u32[]{:S(2)}) collective-permute-start(bf16[384,512]{1,0:T(8,128)(2,1)} %collective-permute-done.8), channel_id=1, source_target_pairs={{0,2},{2,0},{1,3},{3,1},{4,6},{6,4},{5,7},{7,5},{8,10},{10,8},{9,1... | collective-permute-start | bytes 1179656 | tf_op jit(solution)/shard_map/ppermute | solution.py:188
  80.1 11.5 %collective-permute-start.10 = (bf16[384,512]{1,0:T(8,128)(2,1)}, bf16[384,512]{1,0:T(8,128)(2,1)S(1)}, u32[]{:S(2)}, u32[]{:S(2)}) collective-permute-start(bf16[384,512]{1,0:T(8,128)(2,1)} %collective-permute-done.8), channel_id=1, source_target_pairs={{0,224},{32,0},{64,32},{96,64},{128,96},{160,128},{192,160},{224,1... | collective-permute-start | bytes 1179656 | tf_op jit(solution)/shard_map/ppermute | solution.py:26
  82.8 42.1 %collective-permute-start.22 = (bf16[384,512]{1,0:T(8,128)(2,1)}, bf16[384,512]{1,0:T(8,128)(2,1)S(1)}, u32[]{:S(2)}, u32[]{:S(2)}) collective-permute-start(bf16[384,512]{1,0:T(8,128)(2,1)} %collective-permute-done.9), channel_id=1, source_target_pairs={{0,2},{2,0},{1,3},{3,1},{4,6},{6,4},{5,7},{7,5},{8,10},{10,8},{9,1... | collective-permute-start | bytes 1179656 | tf_op jit(solution)/shard_map/ppermute | solution.py:188
  83.1 11.9 %collective-permute-start.11 = (bf16[384,512]{1,0:T(8,128)(2,1)}, bf16[384,512]{1,0:T(8,128)(2,1)S(1)}, u32[]{:S(2)}, u32[]{:S(2)}) collective-permute-start(bf16[384,512]{1,0:T(8,128)(2,1)} %collective-permute-done.9), channel_id=1, source_target_pairs={{0,32},{32,64},{64,96},{96,128},{128,160},{160,192},{192,224},{224... | collective-permute-start | bytes 1179656 | tf_op jit(solution)/shard_map/ppermute | solution.py:26
  95.0 13.8 %collective-permute-start.17 = (bf16[384,512]{1,0:T(8,128)(2,1)S(1)}, bf16[384,512]{1,0:T(8,128)(2,1)S(1)}, u32[]{:S(2)}, u32[]{:S(2)}) collective-permute-start(bf16[384,512]{1,0:T(8,128)(2,1)S(1)} %collective-permute-done.10), channel_id=1, source_target_pairs={{0,2},{2,0},{1,3},{3,1},{4,6},{6,4},{5,7},{7,5},{8,10},{10,8},{9,1... | collective-permute-start | bytes 1179656 | tf_op jit(solution)/shard_map/ppermute | solution.py:188
  96.0 10.7 %collective-permute-start.12 = (bf16[384,512]{1,0:T(8,128)(2,1)S(1)}, bf16[384,512]{1,0:T(8,128)(2,1)S(1)}, u32[]{:S(2)}, u32[]{:S(2)}) collective-permute-start(bf16[384,512]{1,0:T(8,128)(2,1)S(1)} %collective-permute-done.10), channel_id=1, source_target_pairs={{0,224},{32,0},{64,32},{96,64},{128,96},{160,128},{192,160},{224,1... | collective-permute-start | bytes 1179656 | tf_op jit(solution)/shard_map/ppermute | solution.py:26
  96.0 12.0 %collective-permute-start.13 = (bf16[384,512]{1,0:T(8,128)(2,1)S(1)}, bf16[384,512]{1,0:T(8,128)(2,1)S(1)}, u32[]{:S(2)}, u32[]{:S(2)}) collective-permute-start(bf16[384,512]{1,0:T(8,128)(2,1)S(1)} %collective-permute-done.11), channel_id=1, source_target_pairs={{0,32},{32,64},{64,96},{96,128},{128,160},{160,192},{192,224},{224... | collective-permute-start | bytes 1179656 | tf_op jit(solution)/shard_map/ppermute | solution.py:26
  97.5 26.5 %collective-permute-start.21 = (bf16[384,512]{1,0:T(8,128)(2,1)S(1)}, bf16[384,512]{1,0:T(8,128)(2,1)S(1)}, u32[]{:S(2)}, u32[]{:S(2)}) collective-permute-start(bf16[384,512]{1,0:T(8,128)(2,1)S(1)} %collective-permute-done.11), channel_id=1, source_target_pairs={{0,2},{2,0},{1,3},{3,1},{4,6},{6,4},{5,7},{7,5},{8,10},{10,8},{9,1... | collective-permute-start | bytes 1179656 | tf_op jit(solution)/shard_map/ppermute | solution.py:188
  108.0 13.5 %collective-permute-start.18 = (bf16[384,512]{1,0:T(8,128)(2,1)S(1)}, bf16[384,512]{1,0:T(8,128)(2,1)S(1)}, u32[]{:S(2)}, u32[]{:S(2)}) collective-permute-start(bf16[384,512]{1,0:T(8,128)(2,1)S(1)} %collective-permute-done.12), channel_id=1, source_target_pairs={{0,2},{2,0},{1,3},{3,1},{4,6},{6,4},{5,7},{7,5},{8,10},{10,8},{9,1... | collective-permute-start | bytes 1179656 | tf_op jit(solution)/shard_map/ppermute | solution.py:188
  108.8 10.7 %collective-permute-start.14 = (bf16[384,512]{1,0:T(8,128)(2,1)S(1)}, bf16[384,512]{1,0:T(8,128)(2,1)S(1)}, u32[]{:S(2)}, u32[]{:S(2)}) collective-permute-start(bf16[384,512]{1,0:T(8,128)(2,1)S(1)} %collective-permute-done.12), channel_id=1, source_target_pairs={{0,224},{32,0},{64,32},{96,64},{128,96},{160,128},{192,160},{224,1... | collective-permute-start | bytes 1179656 | tf_op jit(solution)/shard_map/ppermute | solution.py:185
  108.8 14.5 %collective-permute-start.20 = (bf16[384,512]{1,0:T(8,128)(2,1)S(1)}, bf16[384,512]{1,0:T(8,128)(2,1)S(1)}, u32[]{:S(2)}, u32[]{:S(2)}) collective-permute-start(bf16[384,512]{1,0:T(8,128)(2,1)S(1)} %collective-permute-done.13), channel_id=1, source_target_pairs={{0,2},{2,0},{1,3},{3,1},{4,6},{6,4},{5,7},{7,5},{8,10},{10,8},{9,1... | collective-permute-start | bytes 1179656 | tf_op jit(solution)/shard_map/ppermute | solution.py:188
  119.5 2.8 %collective-permute-start.19 = (bf16[384,512]{1,0:T(8,128)(2,1)S(1)}, bf16[384,512]{1,0:T(8,128)(2,1)S(1)}, u32[]{:S(2)}, u32[]{:S(2)}) collective-permute-start(bf16[384,512]{1,0:T(8,128)(2,1)S(1)} %collective-permute-done.14), channel_id=1, source_target_pairs={{0,2},{2,0},{1,3},{3,1},{4,6},{6,4},{5,7},{7,5},{8,10},{10,8},{9,1... | collective-permute-start | bytes 1179656 | tf_op jit(solution)/shard_map/ppermute | solution.py:188
  121.4 3.4 %copy-start.2 = (bf16[8,384,512]{2,1,0:T(8,128)(2,1)}, bf16[8,384,512]{2,1,0:T(8,128)(2,1)S(1)}, u32[]{:S(2)}) copy-start(bf16[8,384,512]{2,1,0:T(8,128)(2,1)S(1)} %bitcast_dynamic-update-slice_fusion.8.refs_0_.refs_1_) | copy-start | bytes 9437188
  125.6 1.4 copy-start.1
